TPU v7x, 256 devices: a whole 4x4x8 slice. The times are simulated.
256 devices in a mesh: front: 64 (over z, x, core), col: 4 (over y).
Axes of the slice: x: 4, y: 4, z: 8, core: 2. Of those that a mesh axis runs over, the one named last changes fastest.
Arguments:
- leaf_load: bfloat16 [65536, 2048], P('front', 'col'), may hold values from -6 to 6
- leaf_inverse: bfloat16 [65536, 1024], P(('front', 'col')), may hold values from -0.1875 to 0.1875
- leaf_coupling: bfloat16 [32768, 1024], P('front'), may hold values from -0.1875 to 0.1875
- leaf_rowmap: int32 [64, 512], P('front'), may hold values from 0 to 511, each once within a row
- load_first: bfloat16 [16384, 2048], P('front', 'col'), may hold values from -6 to 6
- load_second: bfloat16 [8192, 2048], P('front', 'col'), may hold values from -6 to 6
- load_third: bfloat16 [4096, 2048], P('front', 'col'), may hold values from -6 to 6
- inverse_first: bfloat16 [16384, 512], P('front'), may hold values from -0.15625 to 0.15625
- inverse_second: bfloat16 [8192, 512], P('front'), may hold values from -0.15625 to 0.15625
- inverse_third: bfloat16 [4096, 512], P('front'), may hold values from -0.15625 to 0.15625
- coupling_first: bfloat16 [512, 16384], P(None, 'front'), may hold values from -0.25 to 0.25
- coupling_second: bfloat16 [512, 8192], P(None, 'front'), may hold values from -0.25 to 0.25
- rowmap_first: int32 [32, 512], replicated, may hold values from 0 to 511, each once within a row
- rowmap_second: int32 [16, 512], replicated, may hold values from 0 to 511, each once within a row
- surface_coupling: bfloat16 [192, 1024, 1024], P('front'), may hold values from -0.125 to 0.125
- neighbor_tiles: int32 [64, 2], replicated, may hold values from 0 to 63, as said below
Outputs:
- volume_solution: bfloat16 [65536, 2048], P('front', 'col')
- surface_tiles: bfloat16 [65536, 2048], P('front', 'col')
- solution_first: bfloat16 [16384, 2048], P('front', 'col')
- solution_second: bfloat16 [8192, 2048], P('front', 'col')
- solution_third: bfloat16 [4096, 2048], P('front', 'col')
Inputs may be any that keep to these rules, and one draw needn't show every extreme that they name: Each row of leaf_rowmap is a permutation of the 512 separator rows. Each row of rowmap_first is a permutation of the 512 separator rows. Each row of rowmap_second is a permutation of the 512 separator rows. `neighbor_tiles`: row f names two different tiles, neither equal to f, each within 2 of f; counting each front's own tile, every tile receives 1 to 5 contributions, and some tile receives 5.
All inputs are finite; a program needn't handle non-finite values.
Results may differ from a plain program's by a relative error of at most 0.015.
Values may be sent and summed in bfloat16 or wider, within the bound.
No kernel may reach another device: no remote copies, remote signals or barrier semaphores. Data moves between devices by JAX's collectives and lax.ppermute only.
A program may use at most 128 MiB of HBM per device.

v0:
```python
import jax
import jax.numpy as jnp
from jax import lax
from jax.sharding import PartitionSpec as P


def from_partner(x, axis, bit):
    return lax.ppermute(x, axis, [(i, i ^ 1 << bit) for i in range(lax.axis_size(axis))])


def from_behind(value, axis, steps):
    count = lax.axis_size(axis)
    leading, last = (max(0, -steps), min(count, count - steps))
    return lax.ppermute(value, axis, [(source, source + steps) for source in range(leading, last)])


def climb_tree(own_term, bit_count):
    for level_bit in range(bit_count):
        own_term = own_term + from_partner(own_term, "front", level_bit)
    return own_term


def spread(row_block, bit_count):
    position = lax.axis_index("front")
    for level_bit in range(bit_count):
        partner = from_partner(row_block, "front", level_bit)
        is_upper = position >> level_bit & 1 == 1
        row_block = jnp.where(
            is_upper,
            jnp.concatenate([partner, row_block], axis=0),
            jnp.concatenate([row_block, partner], axis=0),
        )
    return row_block


def pull_back(coupling, lifted):
    return lax.dot_general(
        coupling, lifted, (((0,), (0,)), ((), ())), preferred_element_type=jnp.float32
    )


def local(
    leaf_load,
    leaf_inverse,
    leaf_coupling,
    leaf_rowmap,
    load_first,
    load_second,
    load_third,
    inverse_first,
    inverse_second,
    inverse_third,
    coupling_first,
    coupling_second,
    rowmap_first,
    rowmap_second,
    surface_coupling,
    neighbor_tiles,
):
    position = lax.axis_index("front")
    front_count = lax.axis_size("front")
    factor = lax.all_gather(leaf_inverse, "col", axis=0, tiled=True)
    first_solve = jnp.dot(factor, leaf_load, preferred_element_type=jnp.float32).astype(
        jnp.bfloat16
    )
    sep_order = leaf_coupling.shape[0]
    panel_cols = leaf_load.shape[1]
    partial_value = jnp.dot(leaf_coupling, first_solve, preferred_element_type=jnp.float32)[
        leaf_rowmap[0]
    ]
    load_list = (load_first, load_second, load_third)
    inverses = (inverse_first, inverse_second, inverse_third)
    couplings = (coupling_first, coupling_second)
    rowmaps = (rowmap_first, rowmap_second)
    solved = []
    for level_index in range(3):
        row_count = load_list[level_index].shape[0]
        offset = position % 2 ** (level_index + 1) * row_count
        embedded = lax.dynamic_update_slice_in_dim(
            jnp.zeros((sep_order, panel_cols), jnp.float32),
            load_list[level_index].astype(jnp.float32),
            offset,
            0,
        )
        right_side = climb_tree(embedded - partial_value, level_index + 1).astype(jnp.bfloat16)
        solution = jnp.dot(
            inverses[level_index], right_side, preferred_element_type=jnp.float32
        ).astype(jnp.bfloat16)
        solved.append(solution)
        if level_index < 2:
            row_map = lax.dynamic_index_in_dim(
                rowmaps[level_index], position >> level_index + 1, 0, keepdims=False
            )
            partial_value = jnp.dot(
                couplings[level_index], solution, preferred_element_type=jnp.float32
            )[row_map]
    parent_rows = solved[2]
    results = [None, None, parent_rows]
    for level_index in (1, 0):
        full_vector = spread(parent_rows, level_index + 2)
        row_map = lax.dynamic_index_in_dim(
            rowmaps[level_index], position >> level_index + 1, 0, keepdims=False
        )
        lifted = jnp.zeros((sep_order, panel_cols), jnp.bfloat16).at[row_map].set(full_vector)
        pieces = pull_back(couplings[level_index], lifted).astype(jnp.bfloat16)
        full_pull = spread(pieces, level_index + 1)
        parent_rows = (
            solved[level_index].astype(jnp.float32)
            - jnp.dot(inverses[level_index], full_pull, preferred_element_type=jnp.float32)
        ).astype(jnp.bfloat16)
        results[level_index] = parent_rows
    full_vector = spread(parent_rows, 1)
    lifted = jnp.zeros((sep_order, panel_cols), jnp.bfloat16).at[leaf_rowmap[0]].set(full_vector)
    pulled = pull_back(leaf_coupling, lifted).astype(jnp.bfloat16)
    volume = (
        first_solve.astype(jnp.float32)
        - jnp.dot(factor, pulled, preferred_element_type=jnp.float32)
    ).astype(jnp.bfloat16)
    contribution = jnp.einsum(
        "stf,fp->stp", surface_coupling, volume, preferred_element_type=jnp.float32
    ).astype(jnp.bfloat16)
    tile_sums = contribution[0].astype(jnp.float32)
    for source in (-2, -1, 1, 2):
        arrived = from_behind(contribution[1:], "front", -source)
        anchor = jnp.clip(position + source, 0, front_count - 1)
        aimed_tiles = lax.dynamic_index_in_dim(neighbor_tiles, anchor, 0, keepdims=False)
        matches = (aimed_tiles == position)[:, None, None]
        tile_sums = tile_sums + jnp.sum(
            jnp.where(matches, arrived.astype(jnp.float32), 0.0), axis=0
        )
    return (volume, tile_sums.astype(jnp.bfloat16), results[0], results[1], results[2])


def solution(mesh):
    return jax.shard_map(
        local,
        mesh=mesh,
        in_specs=(
            P("front", "col"),
            P(("front", "col"), None),
            P("front", None),
            P("front", None),
            P("front", "col"),
            P("front", "col"),
            P("front", "col"),
            P("front", None),
            P("front", None),
            P("front", None),
            P(None, "front"),
            P(None, "front"),
            P(),
            P(),
            P("front", None, None),
            P(),
        ),
        out_specs=(
            P("front", "col"),
            P("front", "col"),
            P("front", "col"),
            P("front", "col"),
            P("front", "col"),
        ),
        check_vma=False,
    )
```

profile of v0, /device:TPU:129, one launch (start us, length us, event | category | flops | bytes accessed | tf_op | source)
XLA Modules:
  0.0 308.0 jit_solution(17618731491071650589)
XLA Ops:
  11.5 33.0 %all-gather.2.cloned.1.call-done = bf16[1024,1024]{1,0:T(8,128)(2,1)} async-done(((bf16[256,1024]{1,0:T(8,128)(2,1)}), bf16[1024,1024]{1,0:T(8,128)(2,1)}) %all-gather.2.cloned.1.call-update) | async-done | bytes 2097168 | tf_op jit(solution)/shard_map/all_gather | solution.py:62
  44.5 2.8 convolution_convert_fusion
  62.2 2.6 collective-permute-done.1
  68.1 21.6 %collective-permute-done.2 = f32[512,512]{1,0:T(8,128)S(1)} collective-permute-done((f32[512,512]{1,0:T(8,128)S(1)}, f32[512,512]{1,0:T(8,128)S(1)}, u32[]{:S(2)}, u32[]{:S(2)}) %collective-permute-start.2) | collective-permute-done | bytes 1048608 | tf_op jit(solution)/shard_map/ppermute | solution.py:8
  100.4 23.2 %collective-permute-done.4 = f32[512,512]{1,0:T(8,128)S(1)} collective-permute-done((f32[512,512]{1,0:T(8,128)S(1)}, f32[512,512]{1,0:T(8,128)S(1)}, u32[]{:S(2)}, u32[]{:S(2)}) %collective-permute-start.4) | collective-permute-done | bytes 1048608 | tf_op jit(solution)/shard_map/ppermute | solution.py:8
  123.8 2.8 collective-permute-start.5
  126.6 22.3 %collective-permute-done.5 = f32[512,512]{1,0:T(8,128)S(1)} collective-permute-done((f32[512,512]{1,0:T(8,128)S(1)}, f32[512,512]{1,0:T(8,128)S(1)}, u32[]{:S(2)}, u32[]{:S(2)}) %collective-permute-start.5) | collective-permute-done | bytes 1048608 | tf_op jit(solution)/shard_map/ppermute | solution.py:8
  153.5 3.5 %collective-permute-done.7 = bf16[128,512]{1,0:T(8,128)(2,1)S(1)} collective-permute-done((bf16[128,512]{1,0:T(8,128)(2,1)S(1)}, bf16[128,512]{1,0:T(8,128)(2,1)S(1)}, u32[]{:S(2)}, u32[]{:S(2)}) %collective-permute-start.7) | collective-permute-done | bytes 131104 | tf_op jit(solution)/shard_map/ppermute | solution.py:8
  157.1 3.0 collective-permute-start.8
  160.1 5.5 %collective-permute-done.8 = bf16[256,512]{1,0:T(8,128)(2,1)S(1)} collective-permute-done((bf16[256,512]{1,0:T(8,128)(2,1)S(1)}, bf16[256,512]{1,0:T(8,128)(2,1)S(1)}, u32[]{:S(2)}, u32[]{:S(2)}) %collective-permute-start.8) | collective-permute-done | bytes 262176 | tf_op jit(solution)/shard_map/ppermute | solution.py:8
  165.5 2.6 scatter_custom_fusion
  172.9 6.3 %collective-permute-done.10 = bf16[256,512]{1,0:T(8,128)(2,1)S(1)} collective-permute-done((bf16[256,512]{1,0:T(8,128)(2,1)S(1)}, bf16[256,512]{1,0:T(8,128)(2,1)S(1)}, u32[]{:S(2)}, u32[]{:S(2)}) %collective-permute-start.10) | collective-permute-done | bytes 262176 | tf_op jit(solution)/shard_map/ppermute | solution.py:8
  183.2 6.3 %collective-permute-done.12 = bf16[256,512]{1,0:T(8,128)(2,1)S(1)} collective-permute-done((bf16[256,512]{1,0:T(8,128)(2,1)S(1)}, bf16[256,512]{1,0:T(8,128)(2,1)S(1)}, u32[]{:S(2)}, u32[]{:S(2)}) %collective-permute-start.12) | collective-permute-done | bytes 262176 | tf_op jit(solution)/shard_map/ppermute | solution.py:8
  189.5 2.6 scatter_custom_fusion.1
  197.0 2.8 scatter_custom_fusion.2
  199.8 4.6 %fusion.4 = bf16[1024,512]{1,0:T(8,128)(2,1)} fusion(bf16[1024,512]{1,0:T(8,128)(2,1)} %copy-done.14, bf16[1024,1024]{1,0:T(8,128)(2,1)} %all-gather.2.cloned.1.call-done, bf16[512,512]{1,0:T(8,128)(2,1)S(1)} %scatter_custom_fusion.2, bf16[512,1024]{1,0:T(8,128)(2,1)S(1)} %copy-done), kind=kOutput, calls=%fused_computation.17 | convolution fusion | flops 1612709888 | bytes 5767168 | tf_op jit(solution)/shard_map/dot_general | solution.py:117
  204.5 6.6 %convert_bitcast_fusion = bf16[3,1024,512]{1,2,0:T(8,128)(2,1)S(1)} fusion(bf16[3,1024,1024]{2,1,0:T(8,128)(2,1)} %param.30, bf16[1024,512]{1,0:T(8,128)(2,1)} %fusion.4), kind=kOutput, calls=%fused_computation.10 | convolution fusion | flops 3222798336 | bytes 10485760 | tf_op jit(solution)/shard_map/stf,fp->stp/dot_general | solution.py:119
  212.7 4.2 %collective-permute-start.18 = (bf16[2,1024,512]{1,2,0:T(8,128)(2,1)S(1)}, bf16[2,1024,512]{1,2,0:T(8,128)(2,1)}, u32[]{:S(2)}, u32[]{:S(2)}) collective-permute-start(bf16[2,1024,512]{1,2,0:T(8,128)(2,1)S(1)} %slice.18), channel_id=1, source_target_pairs={{8,0},{12,4},{16,8},{20,12},{24,16},{28,20},{32,24},{36,28},{40,32... | collective-permute-start | bytes 6291464 | tf_op jit(solution)/shard_map/ppermute | solution.py:14
  219.5 3.0 collective-permute-start.16
  224.7 36.8 %collective-permute-done.18 = bf16[2,1024,512]{1,2,0:T(8,128)(2,1)} collective-permute-done((bf16[2,1024,512]{1,2,0:T(8,128)(2,1)S(1)}, bf16[2,1024,512]{1,2,0:T(8,128)(2,1)}, u32[]{:S(2)}, u32[]{:S(2)}) %collective-permute-start.18) | collective-permute-done | bytes 2097184 | tf_op jit(solution)/shard_map/ppermute | solution.py:14
  261.5 2.6 select_reduce_fusion
  264.1 20.4 %collective-permute-done.17 = bf16[2,1024,512]{1,2,0:T(8,128)(2,1)} collective-permute-done((bf16[2,1024,512]{1,2,0:T(8,128)(2,1)S(1)}, bf16[2,1024,512]{1,2,0:T(8,128)(2,1)}, u32[]{:S(2)}, u32[]{:S(2)}) %collective-permute-start.17) | collective-permute-done | bytes 2097184 | tf_op jit(solution)/shard_map/ppermute | solution.py:14
  287.1 2.6 select_reduce_fusion.2
  289.7 5.2 %collective-permute-done.15 = bf16[2,1024,512]{1,2,0:T(8,128)(2,1)} collective-permute-done((bf16[2,1024,512]{1,2,0:T(8,128)(2,1)S(1)}, bf16[2,1024,512]{1,2,0:T(8,128)(2,1)}, u32[]{:S(2)}, u32[]{:S(2)}) %collective-permute-start.15) | collective-permute-done | bytes 2097184 | tf_op jit(solution)/shard_map/ppermute | solution.py:14
  (98 shorter events, 66.5 us)
Async XLA Ops:
  7.2 41.2 %copy-start = (bf16[512,1024]{1,0:T(8,128)(2,1)S(1)}, bf16[512,1024]{1,0:T(8,128)(2,1)}, u32[]{:S(2)}) copy-start(bf16[512,1024]{1,0:T(8,128)(2,1)} %param.18) | copy-start | bytes 3145732
  7.2 37.4 %copy-start.13 = (bf16[1024,512]{1,0:T(8,128)(2,1)S(1)}, bf16[1024,512]{1,0:T(8,128)(2,1)}, u32[]{:S(2)}) copy-start(bf16[1024,512]{1,0:T(8,128)(2,1)} %param.16) | copy-start | bytes 3145732
  7.2 37.4 %all-gather.2.cloned.1.call-start = ((), (), s32[]{:S(2)}) async-start(), calls=%async_computation | async-start | bytes 2621440 | tf_op jit(solution)/shard_map/all_gather | solution.py:62
  52.6 3.5 %collective-permute-start = (f32[512,512]{1,0:T(8,128)S(1)}, f32[512,512]{1,0:T(8,128)S(1)}, u32[]{:S(2)}, u32[]{:S(2)}) collective-permute-start(f32[512,512]{1,0:T(8,128)S(1)} %sub.20), channel_id=1, source_target_pairs={{0,4},{4,0},{8,12},{12,8},{16,20},{20,16},{24,28},{28,24},{32,36},... | collective-permute-start | bytes 3145736 | tf_op jit(solution)/shard_map/ppermute | solution.py:8
  62.1 2.7 collective-permute-start.1
  65.1 24.7 %collective-permute-start.2 = (f32[512,512]{1,0:T(8,128)S(1)}, f32[512,512]{1,0:T(8,128)S(1)}, u32[]{:S(2)}, u32[]{:S(2)}) collective-permute-start(f32[512,512]{1,0:T(8,128)S(1)} %add.117), channel_id=1, source_target_pairs={{0,8},{4,12},{8,0},{12,4},{16,24},{20,28},{24,16},{28,20},{32,40},... | collective-permute-start | bytes 3145736 | tf_op jit(solution)/shard_map/ppermute | solution.py:8
  95.5 3.4 %collective-permute-start.3 = (f32[512,512]{1,0:T(8,128)S(1)}, f32[512,512]{1,0:T(8,128)S(1)}, u32[]{:S(2)}, u32[]{:S(2)}) collective-permute-start(f32[512,512]{1,0:T(8,128)S(1)} %sub.22), channel_id=1, source_target_pairs={{0,4},{4,0},{8,12},{12,8},{16,20},{20,16},{24,28},{28,24},{32,36},... | collective-permute-start | bytes 3145736 | tf_op jit(solution)/shard_map/ppermute | solution.py:8
  99.1 49.8 %copy-start.11 = (bf16[64,512]{1,0:T(8,128)(2,1)S(1)}, bf16[64,512]{1,0:T(8,128)(2,1)}, u32[]{:S(2)}) copy-start(bf16[64,512]{1,0:T(8,128)(2,1)} %param.25) | copy-start | bytes 196612
  99.1 24.4 %collective-permute-start.4 = (f32[512,512]{1,0:T(8,128)S(1)}, f32[512,512]{1,0:T(8,128)S(1)}, u32[]{:S(2)}, u32[]{:S(2)}) collective-permute-start(f32[512,512]{1,0:T(8,128)S(1)} %add.123), channel_id=1, source_target_pairs={{0,8},{4,12},{8,0},{12,4},{16,24},{20,28},{24,16},{28,20},{32,40},... | collective-permute-start | bytes 3145736 | tf_op jit(solution)/shard_map/ppermute | solution.py:8
  123.8 44.4 %copy-start.3 = (bf16[512,128]{1,0:T(8,128)(2,1)S(1)}, bf16[512,128]{1,0:T(8,128)(2,1)}, u32[]{:S(2)}) copy-start(bf16[512,128]{1,0:T(8,128)(2,1)} %param.27) | copy-start | bytes 393220
  123.8 25.1 %collective-permute-start.5 = (f32[512,512]{1,0:T(8,128)S(1)}, f32[512,512]{1,0:T(8,128)S(1)}, u32[]{:S(2)}, u32[]{:S(2)}) collective-permute-start(f32[512,512]{1,0:T(8,128)S(1)} %add.124), channel_id=1, source_target_pairs={{0,16},{4,20},{8,24},{12,28},{16,0},{20,4},{24,8},{28,12},{32,48},... | collective-permute-start | bytes 3145736 | tf_op jit(solution)/shard_map/ppermute | solution.py:8
  149.2 3.1 collective-permute-start.6
  152.3 4.8 %collective-permute-start.7 = (bf16[128,512]{1,0:T(8,128)(2,1)S(1)}, bf16[128,512]{1,0:T(8,128)(2,1)S(1)}, u32[]{:S(2)}, u32[]{:S(2)}) collective-permute-start(bf16[128,512]{1,0:T(8,128)(2,1)S(1)} %maximum_select_fusion.17), channel_id=1, source_target_pairs={{0,8},{4,12},{8,0},{12,4},{16,24},{20,28},{24,16},{28,20},{32,40},... | collective-permute-start | bytes 393224 | tf_op jit(solution)/shard_map/ppermute | solution.py:8
  157.1 8.4 %collective-permute-start.8 = (bf16[256,512]{1,0:T(8,128)(2,1)S(1)}, bf16[256,512]{1,0:T(8,128)(2,1)S(1)}, u32[]{:S(2)}, u32[]{:S(2)}) collective-permute-start(bf16[256,512]{1,0:T(8,128)(2,1)S(1)} %maximum_select_fusion.14), channel_id=1, source_target_pairs={{0,16},{4,20},{8,24},{12,28},{16,0},{20,4},{24,8},{28,12},{32,48},... | collective-permute-start | bytes 786440 | tf_op jit(solution)/shard_map/ppermute | solution.py:8
  168.4 3.1 %collective-permute-start.9 = (bf16[128,512]{1,0:T(8,128)(2,1)S(1)}, bf16[128,512]{1,0:T(8,128)(2,1)S(1)}, u32[]{:S(2)}, u32[]{:S(2)}) collective-permute-start(bf16[128,512]{1,0:T(8,128)(2,1)S(1)} %fusion.6), channel_id=1, source_target_pairs={{0,4},{4,0},{8,12},{12,8},{16,20},{20,16},{24,28},{28,24},{32,36},... | collective-permute-start | bytes 393224 | tf_op jit(solution)/shard_map/ppermute | solution.py:8
  171.7 7.6 %collective-permute-start.10 = (bf16[256,512]{1,0:T(8,128)(2,1)S(1)}, bf16[256,512]{1,0:T(8,128)(2,1)S(1)}, u32[]{:S(2)}, u32[]{:S(2)}) collective-permute-start(bf16[256,512]{1,0:T(8,128)(2,1)S(1)} %maximum_select_fusion.15), channel_id=1, source_target_pairs={{0,8},{4,12},{8,0},{12,4},{16,24},{20,28},{24,16},{28,20},{32,40},... | collective-permute-start | bytes 786440 | tf_op jit(solution)/shard_map/ppermute | solution.py:8
  179.6 2.3 collective-permute-start.11
  182.0 7.6 %collective-permute-start.12 = (bf16[256,512]{1,0:T(8,128)(2,1)S(1)}, bf16[256,512]{1,0:T(8,128)(2,1)S(1)}, u32[]{:S(2)}, u32[]{:S(2)}) collective-permute-start(bf16[256,512]{1,0:T(8,128)(2,1)S(1)} %maximum_select_fusion.16), channel_id=1, source_target_pairs={{0,8},{4,12},{8,0},{12,4},{16,24},{20,28},{24,16},{28,20},{32,40},... | collective-permute-start | bytes 786440 | tf_op jit(solution)/shard_map/ppermute | solution.py:8
  192.5 2.5 collective-permute-start.13
  195.4 1.6 collective-permute-start.14
  212.7 48.8 %collective-permute-start.18 = (bf16[2,1024,512]{1,2,0:T(8,128)(2,1)S(1)}, bf16[2,1024,512]{1,2,0:T(8,128)(2,1)}, u32[]{:S(2)}, u32[]{:S(2)}) collective-permute-start(bf16[2,1024,512]{1,2,0:T(8,128)(2,1)S(1)} %slice.18), channel_id=1, source_target_pairs={{8,0},{12,4},{16,8},{20,12},{24,16},{28,20},{32,24},{36,28},{40,32... | collective-permute-start | bytes 6291464 | tf_op jit(solution)/shard_map/ppermute | solution.py:14
  216.9 67.6 %collective-permute-start.17 = (bf16[2,1024,512]{1,2,0:T(8,128)(2,1)S(1)}, bf16[2,1024,512]{1,2,0:T(8,128)(2,1)}, u32[]{:S(2)}, u32[]{:S(2)}) collective-permute-start(bf16[2,1024,512]{1,2,0:T(8,128)(2,1)S(1)} %slice.18), channel_id=1, source_target_pairs={{4,0},{8,4},{12,8},{16,12},{20,16},{24,20},{28,24},{32,28},{36,32}... | collective-permute-start | bytes 6291464 | tf_op jit(solution)/shard_map/ppermute | solution.py:14
  219.5 67.6 %collective-permute-start.16 = (bf16[2,1024,512]{1,2,0:T(8,128)(2,1)S(1)}, bf16[2,1024,512]{1,2,0:T(8,128)(2,1)}, u32[]{:S(2)}, u32[]{:S(2)}) collective-permute-start(bf16[2,1024,512]{1,2,0:T(8,128)(2,1)S(1)} %slice.18), channel_id=1, source_target_pairs={{0,4},{4,8},{8,12},{12,16},{16,20},{20,24},{24,28},{28,32},{32,36}... | collective-permute-start | bytes 6291464 | tf_op jit(solution)/shard_map/ppermute | solution.py:14
  222.5 72.3 %collective-permute-start.15 = (bf16[2,1024,512]{1,2,0:T(8,128)(2,1)S(1)}, bf16[2,1024,512]{1,2,0:T(8,128)(2,1)}, u32[]{:S(2)}, u32[]{:S(2)}) collective-permute-start(bf16[2,1024,512]{1,2,0:T(8,128)(2,1)S(1)} %slice.18), channel_id=1, source_target_pairs={{0,8},{4,12},{8,16},{12,20},{16,24},{20,28},{24,32},{28,36},{32,40... | collective-permute-start | bytes 6291464 | tf_op jit(solution)/shard_map/ppermute | solution.py:14
  (11 other events, 154.9 us)
Sparse Core Ops, SparseCore 0:
  9.8 34.6 all-gather.1
where the time goes:
time: 309 us; the launch traced here: 308 us
  waiting for transfers between devices  195 us (63%)
  starting transfers between devices  33.4 us (11%)
  other arithmetic  30.7 us (10%)
  matrix products  21.3 us (7%)
  between operations  14.5 us (5%)
  local copies, waits for them, and re-layouts  13.1 us (4%)
    ppermute x15, waiting for transfers between devices, from_partner(): lax.ppermute(x, axis, [(i, i ^ 1 << bit) for i in range(lax.axis_size(axi...  98.8 us
    ppermute x4, waiting for transfers between devices, from_behind(): lax.ppermute(value, axis, [(source, source + steps) for source in range(l...  62.4 us
    all_gather x1, waiting for transfers between devices, local(): factor = lax.all_gather(leaf_inverse, 'col', axis=0, tiled=True)  33 us
    ppermute x15, starting transfers between devices, from_partner(): lax.ppermute(x, axis, [(i, i ^ 1 << bit) for i in range(lax.axis_size(axi...  21.7 us
    ppermute x4, starting transfers between devices, from_behind(): lax.ppermute(value, axis, [(source, source + steps) for source in range(l...  11.7 us
    reduce_sum x4, other arithmetic, local(): jnp.sum(jnp.where(matches, arrived.astype(jnp.float32), 0.0), axis=0)  10.3 us
    dot_general x1, matrix products, local(): jnp.einsum('stf,fp->stp', surface_coupling, volume, preferred_element_typ...  6.59 us
  transfers between devices with their start and end apart: 20, of which 18 were waited for; matrix products, arithmetic and copies ran while one was open for 5% of the time, Pallas kernels for 0%

commit v1 on v0

--- a/solution.py
+++ b/solution.py
@@ -59,7 +59,9 @@
 ):
     position = lax.axis_index("front")
     front_count = lax.axis_size("front")
-    factor = lax.all_gather(leaf_inverse, "col", axis=0, tiled=True)
+    factor = jnp.concatenate(
+        lax.all_to_all(jnp.stack([leaf_inverse] * lax.axis_size("col")), "col", 0, 0), axis=0
+    )
     first_solve = jnp.dot(factor, leaf_load, preferred_element_type=jnp.float32).astype(
         jnp.bfloat16
     )

time: 309 us -> 296 us (0.958)
  between operations: 14.5 us -> 1.08 us
  waiting for transfers between devices: 195 us -> 184 us
  starting transfers between devices: 33.4 us -> 38.4 us
  local copies, waits for them, and re-layouts: 13.1 us -> 17.8 us
    all_gather x1 -> x0, waiting for transfers between devices: 33 us -> none  [local(): factor = lax.all_gather(leaf_inverse, 'col', axis=0, tiled=True)]
    all_to_all x0 -> x1, waiting for transfers between devices: none -> 23.5 us  [local(): lax.all_to_all(jnp.stack([leaf_inverse] * lax.axis_size('col')), 'col', 0...]
    all_to_all x0 -> x1, starting transfers between devices: none -> 4.31 us  [local(): lax.all_to_all(jnp.stack([leaf_inverse] * lax.axis_size('col')), 'col', 0...]
where the time goes in v1:
time: 296 us; the launch traced here: 295 us
  waiting for transfers between devices  184 us (62%)
  starting transfers between devices  38.4 us (13%)
  other arithmetic  30 us (10%)
  matrix products  23.2 us (8%)
  local copies, waits for them, and re-layouts  17.8 us (6%)
    ppermute x15, waiting for transfers between devices, from_partner(): lax.ppermute(x, axis, [(i, i ^ 1 << bit) for i in range(lax.axis_size(axi...  98.6 us
    ppermute x4, waiting for transfers between devices, from_behind(): lax.ppermute(value, axis, [(source, source + steps) for source in range(l...  62.4 us
    all_to_all x1, waiting for transfers between devices, local(): lax.all_to_all(jnp.stack([leaf_inverse] * lax.axis_size('col')), 'col', 0...  23.5 us
    ppermute x15, starting transfers between devices, from_partner(): lax.ppermute(x, axis, [(i, i ^ 1 << bit) for i in range(lax.axis_size(axi...  22.7 us
    ppermute x4, starting transfers between devices, from_behind(): lax.ppermute(value, axis, [(source, source + steps) for source in range(l...  11.4 us
    reduce_sum x4, other arithmetic, local(): jnp.sum(jnp.where(matches, arrived.astype(jnp.float32), 0.0), axis=0)  10.3 us
    dot_general x1, matrix products, local(): jnp.einsum('stf,fp->stp', surface_coupling, volume, preferred_element_typ...  6.6 us
  transfers between devices with their start and end apart: 20, of which 18 were waited for; matrix products, arithmetic and copies ran while one was open for 5% of the time, Pallas kernels for 0%

profile of v1, /device:TPU:129, one launch (start us, length us, event | category | flops | bytes accessed | tf_op | source)
XLA Modules:
  0.0 295.0 jit_solution(8618200572228767438)
XLA Ops:
  0.6 2.7 stack.2
  3.4 4.3 %all-to-all-start = ((bf16[4,256,1024]{2,1,0:T(8,128)(2,1)}), bf16[4,256,1024]{2,1,0:T(8,128)(2,1)S(1)}, u32[]{:S(2)}, u32[]{:S(2)}) async-start(bf16[4,256,1024]{2,1,0:T(8,128)(2,1)} %stack.2), calls=%async_computation | async-start | bytes 4194304 | tf_op jit(solution)/shard_map/all_to_all | solution.py:63
  9.7 23.5 %all-to-all-done = bf16[4,256,1024]{2,1,0:T(8,128)(2,1)S(1)} async-done(((bf16[4,256,1024]{2,1,0:T(8,128)(2,1)}), bf16[4,256,1024]{2,1,0:T(8,128)(2,1)S(1)}, u32[]{:S(2)}, u32[]{:S(2)}) %all-to-all-start) | async-done | bytes 2097184 | tf_op jit(solution)/shard_map/all_to_all | solution.py:63
  33.2 3.2 %convolution_convert_fusion = bf16[1024,512]{1,0:T(8,128)(2,1)S(1)} fusion(bf16[1024,1024]{1,0:T(8,128)(2,1)S(1)} %bitcast.68, bf16[1024,512]{1,0:T(8,128)(2,1)} %param.16), kind=kOutput, calls=%fused_computation.18 | convolution fusion | flops 1074266112 | bytes 4194304 | tf_op jit(solution)/shard_map/dot_general | solution.py:65
  54.5 2.6 collective-permute-done.1
  60.3 21.6 %collective-permute-done.2 = f32[512,512]{1,0:T(8,128)S(1)} collective-permute-done((f32[512,512]{1,0:T(8,128)S(1)}, f32[512,512]{1,0:T(8,128)S(1)}, u32[]{:S(2)}, u32[]{:S(2)}) %collective-permute-start.2) | collective-permute-done | bytes 1048608 | tf_op jit(solution)/shard_map/ppermute | solution.py:8
  92.6 23.1 %collective-permute-done.4 = f32[512,512]{1,0:T(8,128)S(1)} collective-permute-done((f32[512,512]{1,0:T(8,128)S(1)}, f32[512,512]{1,0:T(8,128)S(1)}, u32[]{:S(2)}, u32[]{:S(2)}) %collective-permute-start.4) | collective-permute-done | bytes 1048608 | tf_op jit(solution)/shard_map/ppermute | solution.py:8
  116.0 2.8 collective-permute-start.5
  118.8 22.2 %collective-permute-done.5 = f32[512,512]{1,0:T(8,128)S(1)} collective-permute-done((f32[512,512]{1,0:T(8,128)S(1)}, f32[512,512]{1,0:T(8,128)S(1)}, u32[]{:S(2)}, u32[]{:S(2)}) %collective-permute-start.5) | collective-permute-done | bytes 1048608 | tf_op jit(solution)/shard_map/ppermute | solution.py:8
  145.8 3.5 %collective-permute-done.7 = bf16[128,512]{1,0:T(8,128)(2,1)S(1)} collective-permute-done((bf16[128,512]{1,0:T(8,128)(2,1)S(1)}, bf16[128,512]{1,0:T(8,128)(2,1)S(1)}, u32[]{:S(2)}, u32[]{:S(2)}) %collective-permute-start.7) | collective-permute-done | bytes 131104 | tf_op jit(solution)/shard_map/ppermute | solution.py:8
  149.3 3.0 %collective-permute-start.8 = (bf16[256,512]{1,0:T(8,128)(2,1)S(1)}, bf16[256,512]{1,0:T(8,128)(2,1)S(1)}, u32[]{:S(2)}, u32[]{:S(2)}) collective-permute-start(bf16[256,512]{1,0:T(8,128)(2,1)S(1)} %maximum_select_fusion.14), channel_id=1, source_target_pairs={{0,16},{4,20},{8,24},{12,28},{16,0},{20,4},{24,8},{28,12},{32,48},... | collective-permute-start | bytes 786440 | tf_op jit(solution)/shard_map/ppermute | solution.py:8
  152.3 5.4 %collective-permute-done.8 = bf16[256,512]{1,0:T(8,128)(2,1)S(1)} collective-permute-done((bf16[256,512]{1,0:T(8,128)(2,1)S(1)}, bf16[256,512]{1,0:T(8,128)(2,1)S(1)}, u32[]{:S(2)}, u32[]{:S(2)}) %collective-permute-start.8) | collective-permute-done | bytes 262176 | tf_op jit(solution)/shard_map/ppermute | solution.py:8
  157.7 2.6 scatter_custom_fusion
  165.2 6.3 %collective-permute-done.10 = bf16[256,512]{1,0:T(8,128)(2,1)S(1)} collective-permute-done((bf16[256,512]{1,0:T(8,128)(2,1)S(1)}, bf16[256,512]{1,0:T(8,128)(2,1)S(1)}, u32[]{:S(2)}, u32[]{:S(2)}) %collective-permute-start.10) | collective-permute-done | bytes 262176 | tf_op jit(solution)/shard_map/ppermute | solution.py:8
  175.4 6.3 %collective-permute-done.12 = bf16[256,512]{1,0:T(8,128)(2,1)S(1)} collective-permute-done((bf16[256,512]{1,0:T(8,128)(2,1)S(1)}, bf16[256,512]{1,0:T(8,128)(2,1)S(1)}, u32[]{:S(2)}, u32[]{:S(2)}) %collective-permute-start.12) | collective-permute-done | bytes 262176 | tf_op jit(solution)/shard_map/ppermute | solution.py:8
  181.7 2.6 scatter_custom_fusion.1
  190.7 3.8 %scatter_custom_fusion.2 = bf16[512,512]{1,0:T(8,128)(2,1)} fusion(s32[512]{0:T(512)S(1)} %bitcast.71, bf16[256,512]{1,0:T(8,128)(2,1)} %copy-done.6, bf16[]{:T(256)} %constant.96, bf16[256,512]{1,0:T(8,128)(2,1)S(1)} %collective-permute-done.14, pred[]{:T(512)S(6)} %eq.65, bf16[]{:T(256)} %constant.70.clone.1), kind=kCustom, calls=%fused_computation.65 | custom fusion | flops 2359296 | bytes 1048581 | tf_op jit(solution)/shard_map/scatter | solution.py:115
  194.5 4.2 %fusion.4 = bf16[1024,512]{1,0:T(8,128)(2,1)} fusion(bf16[1024,512]{1,0:T(8,128)(2,1)} %copy-done.16, bf16[1024,1024]{1,0:T(8,128)(2,1)S(1)} %bitcast.69, bf16[512,512]{1,0:T(8,128)(2,1)} %scatter_custom_fusion.2, bf16[512,1024]{1,0:T(8,128)(2,1)S(1)} %copy-done), kind=kOutput, calls=%fused_computation.17 | convolution fusion | flops 1612709888 | bytes 5767168 | tf_op jit(solution)/shard_map/dot_general | solution.py:119
  198.7 6.6 %convert_bitcast_fusion = bf16[3,1024,512]{1,2,0:T(8,128)(2,1)S(1)} fusion(bf16[3,1024,1024]{2,1,0:T(8,128)(2,1)} %param.30, bf16[1024,512]{1,0:T(8,128)(2,1)} %fusion.4), kind=kOutput, calls=%fused_computation.10 | convolution fusion | flops 3222798336 | bytes 10485760 | tf_op jit(solution)/shard_map/stf,fp->stp/dot_general | solution.py:121
  206.9 3.9 %collective-permute-start.18 = (bf16[2,1024,512]{1,2,0:T(8,128)(2,1)S(1)}, bf16[2,1024,512]{1,2,0:T(8,128)(2,1)}, u32[]{:S(2)}, u32[]{:S(2)}) collective-permute-start(bf16[2,1024,512]{1,2,0:T(8,128)(2,1)S(1)} %slice.18), channel_id=1, source_target_pairs={{8,0},{12,4},{16,8},{20,12},{24,16},{28,20},{32,24},{36,28},{40,32... | collective-permute-start | bytes 6291464 | tf_op jit(solution)/shard_map/ppermute | solution.py:14
  213.4 3.0 %collective-permute-start.16 = (bf16[2,1024,512]{1,2,0:T(8,128)(2,1)S(1)}, bf16[2,1024,512]{1,2,0:T(8,128)(2,1)}, u32[]{:S(2)}, u32[]{:S(2)}) collective-permute-start(bf16[2,1024,512]{1,2,0:T(8,128)(2,1)S(1)} %slice.18), channel_id=1, source_target_pairs={{0,4},{4,8},{8,12},{12,16},{16,20},{20,24},{24,28},{28,32},{32,36}... | collective-permute-start | bytes 6291464 | tf_op jit(solution)/shard_map/ppermute | solution.py:14
  218.6 37.1 %collective-permute-done.18 = bf16[2,1024,512]{1,2,0:T(8,128)(2,1)} collective-permute-done((bf16[2,1024,512]{1,2,0:T(8,128)(2,1)S(1)}, bf16[2,1024,512]{1,2,0:T(8,128)(2,1)}, u32[]{:S(2)}, u32[]{:S(2)}) %collective-permute-start.18) | collective-permute-done | bytes 2097184 | tf_op jit(solution)/shard_map/ppermute | solution.py:14
  258.3 20.4 %collective-permute-done.17 = bf16[2,1024,512]{1,2,0:T(8,128)(2,1)} collective-permute-done((bf16[2,1024,512]{1,2,0:T(8,128)(2,1)S(1)}, bf16[2,1024,512]{1,2,0:T(8,128)(2,1)}, u32[]{:S(2)}, u32[]{:S(2)}) %collective-permute-start.17) | collective-permute-done | bytes 2097184 | tf_op jit(solution)/shard_map/ppermute | solution.py:14
  283.9 4.8 %collective-permute-done.15 = bf16[2,1024,512]{1,2,0:T(8,128)(2,1)} collective-permute-done((bf16[2,1024,512]{1,2,0:T(8,128)(2,1)S(1)}, bf16[2,1024,512]{1,2,0:T(8,128)(2,1)}, u32[]{:S(2)}, u32[]{:S(2)}) %collective-permute-start.15) | collective-permute-done | bytes 2097184 | tf_op jit(solution)/shard_map/ppermute | solution.py:14
  (102 shorter events, 74.1 us)
Async XLA Ops:
  0.6 36.8 %copy-start = (bf16[512,1024]{1,0:T(8,128)(2,1)S(1)}, bf16[512,1024]{1,0:T(8,128)(2,1)}, u32[]{:S(2)}) copy-start(bf16[512,1024]{1,0:T(8,128)(2,1)} %param.18) | copy-start | bytes 3145732
  3.4 29.8 %all-to-all-start = ((bf16[4,256,1024]{2,1,0:T(8,128)(2,1)}), bf16[4,256,1024]{2,1,0:T(8,128)(2,1)S(1)}, u32[]{:S(2)}, u32[]{:S(2)}) async-start(bf16[4,256,1024]{2,1,0:T(8,128)(2,1)} %stack.2), calls=%async_computation | async-start | bytes 4194304 | tf_op jit(solution)/shard_map/all_to_all | solution.py:63
  43.8 4.5 %collective-permute-start = (f32[512,512]{1,0:T(8,128)S(1)}, f32[512,512]{1,0:T(8,128)S(1)}, u32[]{:S(2)}, u32[]{:S(2)}) collective-permute-start(f32[512,512]{1,0:T(8,128)S(1)} %sub.20), channel_id=1, source_target_pairs={{0,4},{4,0},{8,12},{12,8},{16,20},{20,16},{24,28},{28,24},{32,36},... | collective-permute-start | bytes 3145736 | tf_op jit(solution)/shard_map/ppermute | solution.py:8
  54.3 2.7 collective-permute-start.1
  57.3 24.7 %collective-permute-start.2 = (f32[512,512]{1,0:T(8,128)S(1)}, f32[512,512]{1,0:T(8,128)S(1)}, u32[]{:S(2)}, u32[]{:S(2)}) collective-permute-start(f32[512,512]{1,0:T(8,128)S(1)} %add.117), channel_id=1, source_target_pairs={{0,8},{4,12},{8,0},{12,4},{16,24},{20,28},{24,16},{28,20},{32,40},... | collective-permute-start | bytes 3145736 | tf_op jit(solution)/shard_map/ppermute | solution.py:8
  87.7 3.4 %collective-permute-start.3 = (f32[512,512]{1,0:T(8,128)S(1)}, f32[512,512]{1,0:T(8,128)S(1)}, u32[]{:S(2)}, u32[]{:S(2)}) collective-permute-start(f32[512,512]{1,0:T(8,128)S(1)} %sub.22), channel_id=1, source_target_pairs={{0,4},{4,0},{8,12},{12,8},{16,20},{20,16},{24,28},{28,24},{32,36},... | collective-permute-start | bytes 3145736 | tf_op jit(solution)/shard_map/ppermute | solution.py:8
  91.3 49.8 %copy-start.13 = (bf16[64,512]{1,0:T(8,128)(2,1)S(1)}, bf16[64,512]{1,0:T(8,128)(2,1)}, u32[]{:S(2)}) copy-start(bf16[64,512]{1,0:T(8,128)(2,1)} %param.25) | copy-start | bytes 196612
  91.3 24.4 %collective-permute-start.4 = (f32[512,512]{1,0:T(8,128)S(1)}, f32[512,512]{1,0:T(8,128)S(1)}, u32[]{:S(2)}, u32[]{:S(2)}) collective-permute-start(f32[512,512]{1,0:T(8,128)S(1)} %add.123), channel_id=1, source_target_pairs={{0,8},{4,12},{8,0},{12,4},{16,24},{20,28},{24,16},{28,20},{32,40},... | collective-permute-start | bytes 3145736 | tf_op jit(solution)/shard_map/ppermute | solution.py:8
  116.0 44.4 %copy-start.5 = (bf16[512,128]{1,0:T(8,128)(2,1)S(1)}, bf16[512,128]{1,0:T(8,128)(2,1)}, u32[]{:S(2)}) copy-start(bf16[512,128]{1,0:T(8,128)(2,1)} %param.27) | copy-start | bytes 393220
  116.0 25.1 %collective-permute-start.5 = (f32[512,512]{1,0:T(8,128)S(1)}, f32[512,512]{1,0:T(8,128)S(1)}, u32[]{:S(2)}, u32[]{:S(2)}) collective-permute-start(f32[512,512]{1,0:T(8,128)S(1)} %add.124), channel_id=1, source_target_pairs={{0,16},{4,20},{8,24},{12,28},{16,0},{20,4},{24,8},{28,12},{32,48},... | collective-permute-start | bytes 3145736 | tf_op jit(solution)/shard_map/ppermute | solution.py:8
  141.3 30.4 %copy-start.7 = (bf16[64,512]{1,0:T(8,128)(2,1)}, bf16[64,512]{1,0:T(8,128)(2,1)S(1)}, u32[]{:S(2)}) copy-start(bf16[64,512]{1,0:T(8,128)(2,1)S(1)} %fusion.7) | copy-start | bytes 196612
  141.4 3.1 %collective-permute-start.6 = (bf16[64,512]{1,0:T(8,128)(2,1)S(1)}, bf16[64,512]{1,0:T(8,128)(2,1)S(1)}, u32[]{:S(2)}, u32[]{:S(2)}) collective-permute-start(bf16[64,512]{1,0:T(8,128)(2,1)S(1)} %fusion.7), channel_id=1, source_target_pairs={{0,4},{4,0},{8,12},{12,8},{16,20},{20,16},{24,28},{28,24},{32,36},... | collective-permute-start | bytes 196616 | tf_op jit(solution)/shard_map/ppermute | solution.py:8
  144.5 4.8 %collective-permute-start.7 = (bf16[128,512]{1,0:T(8,128)(2,1)S(1)}, bf16[128,512]{1,0:T(8,128)(2,1)S(1)}, u32[]{:S(2)}, u32[]{:S(2)}) collective-permute-start(bf16[128,512]{1,0:T(8,128)(2,1)S(1)} %maximum_select_fusion.17), channel_id=1, source_target_pairs={{0,8},{4,12},{8,0},{12,4},{16,24},{20,28},{24,16},{28,20},{32,40},... | collective-permute-start | bytes 393224 | tf_op jit(solution)/shard_map/ppermute | solution.py:8
  149.3 8.4 %collective-permute-start.8 = (bf16[256,512]{1,0:T(8,128)(2,1)S(1)}, bf16[256,512]{1,0:T(8,128)(2,1)S(1)}, u32[]{:S(2)}, u32[]{:S(2)}) collective-permute-start(bf16[256,512]{1,0:T(8,128)(2,1)S(1)} %maximum_select_fusion.14), channel_id=1, source_target_pairs={{0,16},{4,20},{8,24},{12,28},{16,0},{20,4},{24,8},{28,12},{32,48},... | collective-permute-start | bytes 786440 | tf_op jit(solution)/shard_map/ppermute | solution.py:8
  160.7 3.1 %collective-permute-start.9 = (bf16[128,512]{1,0:T(8,128)(2,1)S(1)}, bf16[128,512]{1,0:T(8,128)(2,1)S(1)}, u32[]{:S(2)}, u32[]{:S(2)}) collective-permute-start(bf16[128,512]{1,0:T(8,128)(2,1)S(1)} %fusion.6), channel_id=1, source_target_pairs={{0,4},{4,0},{8,12},{12,8},{16,20},{20,16},{24,28},{28,24},{32,36},... | collective-permute-start | bytes 393224 | tf_op jit(solution)/shard_map/ppermute | solution.py:8
  163.9 7.6 %collective-permute-start.10 = (bf16[256,512]{1,0:T(8,128)(2,1)S(1)}, bf16[256,512]{1,0:T(8,128)(2,1)S(1)}, u32[]{:S(2)}, u32[]{:S(2)}) collective-permute-start(bf16[256,512]{1,0:T(8,128)(2,1)S(1)} %maximum_select_fusion.15), channel_id=1, source_target_pairs={{0,8},{4,12},{8,0},{12,4},{16,24},{20,28},{24,16},{28,20},{32,40},... | collective-permute-start | bytes 786440 | tf_op jit(solution)/shard_map/ppermute | solution.py:8
  171.8 2.3 collective-permute-start.11
  174.2 7.6 %collective-permute-start.12 = (bf16[256,512]{1,0:T(8,128)(2,1)S(1)}, bf16[256,512]{1,0:T(8,128)(2,1)S(1)}, u32[]{:S(2)}, u32[]{:S(2)}) collective-permute-start(bf16[256,512]{1,0:T(8,128)(2,1)S(1)} %maximum_select_fusion.16), channel_id=1, source_target_pairs={{0,8},{4,12},{8,0},{12,4},{16,24},{20,28},{24,16},{28,20},{32,40},... | collective-permute-start | bytes 786440 | tf_op jit(solution)/shard_map/ppermute | solution.py:8
  184.7 2.5 collective-permute-start.13
  189.2 1.5 collective-permute-start.14
  206.9 48.8 %collective-permute-start.18 = (bf16[2,1024,512]{1,2,0:T(8,128)(2,1)S(1)}, bf16[2,1024,512]{1,2,0:T(8,128)(2,1)}, u32[]{:S(2)}, u32[]{:S(2)}) collective-permute-start(bf16[2,1024,512]{1,2,0:T(8,128)(2,1)S(1)} %slice.18), channel_id=1, source_target_pairs={{8,0},{12,4},{16,8},{20,12},{24,16},{28,20},{32,24},{36,28},{40,32... | collective-permute-start | bytes 6291464 | tf_op jit(solution)/shard_map/ppermute | solution.py:14
  210.8 67.9 %collective-permute-start.17 = (bf16[2,1024,512]{1,2,0:T(8,128)(2,1)S(1)}, bf16[2,1024,512]{1,2,0:T(8,128)(2,1)}, u32[]{:S(2)}, u32[]{:S(2)}) collective-permute-start(bf16[2,1024,512]{1,2,0:T(8,128)(2,1)S(1)} %slice.18), channel_id=1, source_target_pairs={{4,0},{8,4},{12,8},{16,12},{20,16},{24,20},{28,24},{32,28},{36,32}... | collective-permute-start | bytes 6291464 | tf_op jit(solution)/shard_map/ppermute | solution.py:14
  213.4 67.9 %collective-permute-start.16 = (bf16[2,1024,512]{1,2,0:T(8,128)(2,1)S(1)}, bf16[2,1024,512]{1,2,0:T(8,128)(2,1)}, u32[]{:S(2)}, u32[]{:S(2)}) collective-permute-start(bf16[2,1024,512]{1,2,0:T(8,128)(2,1)S(1)} %slice.18), channel_id=1, source_target_pairs={{0,4},{4,8},{8,12},{12,16},{16,20},{20,24},{24,28},{28,32},{32,36}... | collective-permute-start | bytes 6291464 | tf_op jit(solution)/shard_map/ppermute | solution.py:14
  216.4 72.3 %collective-permute-start.15 = (bf16[2,1024,512]{1,2,0:T(8,128)(2,1)S(1)}, bf16[2,1024,512]{1,2,0:T(8,128)(2,1)}, u32[]{:S(2)}, u32[]{:S(2)}) collective-permute-start(bf16[2,1024,512]{1,2,0:T(8,128)(2,1)S(1)} %slice.18), channel_id=1, source_target_pairs={{0,8},{4,12},{8,16},{12,20},{16,24},{20,28},{24,32},{28,36},{32,40... | collective-permute-start | bytes 6291464 | tf_op jit(solution)/shard_map/ppermute | solution.py:14
  (13 other events, 104.0 us)
